TPU v7x, 512 devices: a whole 4x4x16 slice. The times are simulated.
512 devices in a mesh: frame: 16 (over z), dom: 8 (over x, core), coef: 4 (over y).
Axes of the slice: x: 4, y: 4, z: 16, core: 2. Of those that a mesh axis runs over, the one named last changes fastest.
Arguments:
- geometry: float32 [32, 524288], P('coef', ('frame', 'dom')), may hold values from -1 to 1
- fraction: float32 [32, 524288], P('coef', ('frame', 'dom')), may hold values from 0 to 1
- interval: int32 [32, 524288], P('coef', ('frame', 'dom')), may hold values from 0 to 156
- pattern: int32 [32, 4096], P('coef', ('frame', 'dom')), may hold values from 0 to 95
- target: float32 [524288], P(('frame', 'dom')), may hold values from -8 to 8
Outputs:
- solution: float32 [384, 160], P('coef')
- residual: float32 [524288], P(('frame', 'dom'))
Inputs may be any that keep to these rules, and one draw needn't show every extreme that they name: The spline of a slot reads coefficients interval to interval + 3 of its type. Slot s refers to pair type (s // 8) * 96 + pattern.
All inputs are finite; a program needn't handle non-finite values.
Results may differ from a plain program's by a relative error of at most 0.0003.
Values sent between devices are 32-bit elements; how exact they have to be, the bound alone decides.
No kernel may reach another device: no remote copies, remote signals or barrier semaphores. Data moves between devices by JAX's collectives and lax.ppermute only.
A program may use at most 64 MiB of HBM per device.

v0:
```python
import math
import jax
import jax.numpy as jnp
from jax import lax
from jax.sharding import PartitionSpec as P

NK = 160
TYPES = 384
ITERS = 2


def spline_weights(fraction):
    square = fraction * fraction
    cube = square * fraction
    return (
        (1.0 - fraction) ** 3 / 6.0,
        (3.0 * cube - 6.0 * square + 4.0) / 6.0,
        (-3.0 * cube + 3.0 * square + 3.0 * fraction + 1.0) / 6.0,
        cube / 6.0,
    )


def dense_tiles(geom, fraction, interval):
    knots = lax.broadcasted_iota(jnp.int32, (1, NK, 1), 1)
    tiles = jnp.zeros((geom.shape[0], NK, geom.shape[1]), jnp.float32)
    for offset, weight in enumerate(spline_weights(fraction)):
        hit = knots == (interval + offset)[:, None, :]
        tiles = tiles + jnp.where(hit, (geom * weight)[:, None, :], 0.0)
    return tiles


def block_layout(geom):
    tiles_all = geom.shape[1] // 128
    block = math.gcd(8, tiles_all)
    return (block, block * 128, tiles_all // block)


def block_tiles(geometry, fraction, interval, pattern, index, block, width):
    start = index * width
    geom = lax.dynamic_slice_in_dim(geometry, start, width, 1)
    frac = lax.dynamic_slice_in_dim(fraction, start, width, 1)
    knot = lax.dynamic_slice_in_dim(interval, start, width, 1)
    kinds = lax.dynamic_slice_in_dim(pattern, index * block, block, 1)
    tiles = dense_tiles(geom, frac, knot).reshape(geom.shape[0], NK, block, 128)
    return (tiles, kinds, start)


def forward(coeffs, geometry, fraction, interval, pattern):
    block, width, count = block_layout(geometry)

    def forward_step(index, image):
        tiles, kinds, start = block_tiles(
            geometry, fraction, interval, pattern, index, block, width
        )
        chosen = jnp.take(coeffs, kinds, axis=0)
        part = jnp.einsum("sktr,stk->tr", tiles, chosen, precision=lax.Precision.HIGHEST)
        return lax.dynamic_update_slice_in_dim(image, part.reshape(width), start, 0)

    return lax.fori_loop(0, count, forward_step, jnp.zeros((geometry.shape[1],), jnp.float32))


def backward(resid, per_coef, geometry, fraction, interval, pattern):
    block, width, count = block_layout(geometry)
    owners = lax.broadcasted_iota(jnp.int32, (1, 1, per_coef), 2)

    def backward_step(index, total):
        tiles, kinds, start = block_tiles(
            geometry, fraction, interval, pattern, index, block, width
        )
        piece = lax.dynamic_slice_in_dim(resid, start, width, 0).reshape(block, 128)
        contrib = jnp.einsum("sktr,tr->stk", tiles, piece, precision=lax.Precision.HIGHEST)
        picks = (kinds[:, :, None] == owners).astype(jnp.float32)
        return total + jnp.einsum("stc,stk->ck", picks, contrib, precision=lax.Precision.HIGHEST)

    return lax.fori_loop(0, count, backward_step, jnp.zeros((per_coef, NK), jnp.float32))


def on_device(geometry, fraction, interval, pattern, target):
    per_coef = TYPES // lax.axis_size("coef")

    def transpose_sum(resid):
        local = backward(resid, per_coef, geometry, fraction, interval, pattern).reshape(
            per_coef * NK
        )
        share = lax.psum(local, ("frame", "dom"))
        total = lax.psum(jnp.sum(share * share), "coef")
        return (share, total)

    def expand(share):
        return share.reshape(per_coef, NK)

    residual = target
    gradient, gamma = transpose_sum(residual)
    direction = gradient
    solution = jnp.zeros_like(gradient)
    for step_index in range(ITERS):
        partial_image = forward(expand(direction), geometry, fraction, interval, pattern)
        image = lax.psum(partial_image, "coef")
        image_total = lax.psum(jnp.sum(image * image), ("frame", "dom"))
        alpha = gamma / image_total
        solution = solution + alpha * direction
        residual = residual - alpha * image
        if step_index + 1 < ITERS:
            gradient, gamma_next = transpose_sum(residual)
            direction = gradient + gamma_next / gamma * direction
            gamma = gamma_next
    return (expand(solution), residual)


def solution(mesh):
    in_specs = (
        P("coef", ("frame", "dom")),
        P("coef", ("frame", "dom")),
        P("coef", ("frame", "dom")),
        P("coef", ("frame", "dom")),
        P(("frame", "dom")),
    )
    out_specs = (P("coef", None), P(("frame", "dom")))
    return jax.shard_map(
        on_device, mesh=mesh, in_specs=in_specs, out_specs=out_specs, check_vma=False
    )
```

profile of v0, /device:TPU:1, one launch (start us, length us, event | category | flops | bytes accessed | tf_op | source)
XLA Modules:
  0.0 1750.1 jit_solution(9884929640221820795)
XLA Ops:
  0.6 52.4 %while.56 = (s32[]{:T(128)}, f32[96,160]{0,1:T(8,128)S(1)}, s32[8,32]{1,0:T(8,128)}, f32[4096]{0:T(1024)}, s32[8,4096]{1,0:T(8,128)}, /*index=5*/f32[8,4096]{1,0...) while((s32[]{:T(128)}, f32[96,160]{0,1:T(8,128)S(1)}, ...), condition=%wide.region_1.2_spmd.clone, body=%wide.region_0.1_spmd.clone.sunk | while | flops 42192900 | bytes 11854863 | solution.py:75
  0.7 0.8 fusion.117
  2.4 1.9 select_add_fusion.10
  5.0 8.4 fusion.118
  13.8 0.8 fusion.117
  15.5 1.9 select_add_fusion.10
  18.1 8.4 fusion.118
  26.9 0.8 fusion.117
  28.6 1.9 select_add_fusion.10
  31.2 8.4 fusion.118
  41.7 1.9 select_add_fusion.10
  44.3 8.4 fusion.118
  53.3 498.0 %psum.56 = f32[15360]{0:T(1024)S(1)} all-reduce(f32[15360]{0:T(1024)S(1)} %reshape.226), channel_id=1, replica_groups=mesh['frame'=16,'dom'=8,'coef'=4] {'frame','dom'}, use_global_device_ids=true, to_apply=%region_2.3 | all-reduce | flops 15360 | bytes 122880 | tf_op jit(solution)/shard_map/psum | solution.py:85
  551.4 53.3 %while.54 = (s32[]{:T(128)}, f32[4096]{0:T(1024)S(1)}, s32[8,4096]{1,0:T(8,128)}, f32[8,4096]{1,0:T(8,128)}, f32[8,4096]{1,0:T(8,128)}, /*index=5*/s32[8,32]{1,0...) while((s32[]{:T(128)}, f32[4096]{0:T(1024)S(1)}, ...), condition=%wide.region_6.0_spmd, body=%wide.region_5.7_spmd.sunk | while | flops 30371208 | bytes 11859845 | solution.py:59
  553.2 4.2 select_add_fusion.8
  558.3 6.1 fusion.108
  566.5 4.2 select_add_fusion.8
  571.6 6.1 fusion.108
  578.1 0.8 fusion.106
  579.8 4.2 select_add_fusion.8
  585.0 6.1 fusion.108
  593.1 4.2 select_add_fusion.8
  598.3 6.1 fusion.108
  605.3 14.6 all-reduce
  620.5 256.4 %psum.59 = f32[]{:T(128)} all-reduce(f32[]{:T(128)} %multiply_reduce_fusion.3), channel_id=1, replica_groups=mesh['frame'=16,'dom'=8,'coef'=4] {'frame','dom'}, use_global_device_ids=true, to_apply=%region_9.11 | all-reduce | flops 1 | bytes 8 | tf_op jit(solution)/shard_map/psum | solution.py:99
  878.3 49.7 %while.57 = (s32[]{:T(128)}, f32[96,160]{0,1:T(8,128)S(1)}, s32[8,32]{1,0:T(8,128)}, f32[4096]{0:T(1024)S(1)}, s32[8,4096]{1,0:T(8,128)}, /*index=5*/f32[8,4096]...) while((s32[]{:T(128)}, f32[96,160]{0,1:T(8,128)S(1)}, ...), condition=%wide.region_11.13_spmd.clone, body=%wide.region_10.12_spmd.clone.sunk | while | flops 42192900 | bytes 11854863 | solution.py:75
  880.1 1.9 select_add_fusion.11
  882.0 8.4 fusion.124
  892.5 1.9 select_add_fusion.11
  894.4 8.4 fusion.124
  904.9 1.9 select_add_fusion.11
  906.9 8.4 fusion.124
  917.3 1.9 select_add_fusion.11
  919.3 8.4 fusion.124
  928.3 485.9 %psum.60 = f32[15360]{0:T(1024)S(1)} all-reduce(f32[15360]{0:T(1024)S(1)} %reshape.228), channel_id=1, replica_groups=mesh['frame'=16,'dom'=8,'coef'=4] {'frame','dom'}, use_global_device_ids=true, to_apply=%region_12.14 | all-reduce | flops 15360 | bytes 122880 | tf_op jit(solution)/shard_map/psum | solution.py:85
  1414.8 6.9 psum.61
  1423.1 53.3 %while.55 = (s32[]{:T(128)}, f32[4096]{0:T(1024)S(1)}, s32[8,4096]{1,0:T(8,128)}, f32[8,4096]{1,0:T(8,128)}, f32[8,4096]{1,0:T(8,128)}, /*index=5*/s32[8,32]{1,0...) while((s32[]{:T(128)}, f32[4096]{0:T(1024)S(1)}, ...), condition=%wide.region_16.18_spmd, body=%wide.region_15.17_spmd.sunk | while | flops 30371208 | bytes 11859845 | solution.py:59
  1424.8 4.2 select_add_fusion.9
  1430.0 6.1 fusion.113
  1436.4 0.8 fusion.111
  1438.2 4.2 select_add_fusion.9
  1443.3 6.1 fusion.113
  1451.5 4.2 select_add_fusion.9
  1456.6 6.1 fusion.113
  1464.8 4.2 select_add_fusion.9
  1470.0 6.1 fusion.113
  1476.4 12.1 psum.62
  1489.1 258.2 %psum.63 = f32[]{:T(128)} all-reduce(f32[]{:T(128)} %multiply_reduce_fusion.2), channel_id=1, replica_groups=mesh['frame'=16,'dom'=8,'coef'=4] {'frame','dom'}, use_global_device_ids=true, to_apply=%region_19.21 | all-reduce | flops 1 | bytes 8 | tf_op jit(solution)/shard_map/psum | solution.py:99
  (281 shorter events, 42.3 us)
Async XLA Ops:
  4.3 9.1 copy-start
  17.4 9.1 copy-start
  30.5 9.1 copy-start
  43.6 9.1 copy-start
  551.4 326.9 %copy-start.4 = (f32[4096]{0:T(1024)S(1)}, f32[4096]{0:T(1024)}, u32[]{:S(2)}) copy-start(f32[4096]{0:T(1024)} %get-tuple-element.1094) | copy-start | bytes 49156
  551.4 6.0 copy-start.1
  564.8 6.0 copy-start.1
  578.1 6.0 copy-start.1
  591.4 6.0 copy-start.1
  882.0 8.4 copy-start.2
  894.4 8.4 copy-start.2
  906.8 8.4 copy-start.2
  919.3 8.4 copy-start.2
  1423.1 6.0 copy-start.3
  1436.4 6.0 copy-start.3
  1449.8 6.0 copy-start.3
  1463.1 6.0 copy-start.3
where the time goes:
time: 1750 us
  blocking collectives  1530 us (87%)
  matrix products  118 us (7%)
  other arithmetic  78.9 us (5%)
    psum x2, blocking collectives, transpose_sum(): share = lax.psum(local, ('frame', 'dom'))  984 us
    psum x2, blocking collectives, on_device(): image_total = lax.psum(jnp.sum(image * image), ('frame', 'dom'))  515 us
    dot_general x8, matrix products, backward_step(): jnp.einsum('sktr,tr->stk', tiles, piece, precision=lax.Precision.HIGHEST)  66.9 us
    add x16, other arithmetic, dense_tiles(): tiles = tiles + jnp.where(hit, (geom * weight)[:, None, :], 0.0)  49.2 us
    dot_general x8, matrix products, forward_step(): jnp.einsum('sktr,stk->tr', tiles, chosen, precision=lax.Precision.HIGHEST)  49 us

commit v1 on v0

--- a/solution.py
+++ b/solution.py
@@ -82,7 +82,9 @@
         local = backward(resid, per_coef, geometry, fraction, interval, pattern).reshape(
             per_coef * NK
         )
-        share = lax.psum(local, ("frame", "dom"))
+        share = local
+        for mesh_axis in ("frame", "dom"):
+            share = lax.psum(share, mesh_axis)
         total = lax.psum(jnp.sum(share * share), "coef")
         return (share, total)
 

time: 1750 us -> 923 us (0.53)
  blocking collectives: 1530 us -> 702 us
    psum x2 -> x4, blocking collectives: 984 us -> 159 us  [transpose_sum(): share = lax.psum(share, mesh_axis)]
where the time goes in v1:
time: 923 us; the launch traced here: 920 us
  blocking collectives  702 us (76%)
  matrix products  118 us (13%)
  other arithmetic  78.9 us (9%)
  local copies, waits for them, and re-layouts  14.3 us (2%)
    psum x2, blocking collectives, on_device(): image_total = lax.psum(jnp.sum(image * image), ('frame', 'dom'))  510 us
    psum x4, blocking collectives, transpose_sum(): share = lax.psum(share, mesh_axis)  159 us
    dot_general x8, matrix products, backward_step(): jnp.einsum('sktr,tr->stk', tiles, piece, precision=lax.Precision.HIGHEST)  66.9 us
    add x16, other arithmetic, dense_tiles(): tiles = tiles + jnp.where(hit, (geom * weight)[:, None, :], 0.0)  49.2 us
    dot_general x8, matrix products, forward_step(): jnp.einsum('sktr,stk->tr', tiles, chosen, precision=lax.Precision.HIGHEST)  49 us
    psum x2, blocking collectives, on_device(): image = lax.psum(partial_image, 'coef')  27.1 us

profile of v1, /device:TPU:1, one launch (start us, length us, event | category | flops | bytes accessed | tf_op | source)
XLA Modules:
  0.0 920.1 jit_solution(1691553866125200107)
XLA Ops:
  0.6 52.4 %while.56 = (s32[]{:T(128)}, f32[96,160]{0,1:T(8,128)S(1)}, s32[8,32]{1,0:T(8,128)}, f32[4096]{0:T(1024)}, s32[8,4096]{1,0:T(8,128)}, /*index=5*/f32[8,4096]{1,0...) while((s32[]{:T(128)}, f32[96,160]{0,1:T(8,128)S(1)}, ...), condition=%wide.region_1.2_spmd.clone, body=%wide.region_0.1_spmd.clone.sunk | while | flops 42192900 | bytes 11854863 | solution.py:75
  0.7 0.8 fusion.117
  2.4 1.9 select_add_fusion.10
  5.0 8.4 fusion.118
  15.5 1.9 select_add_fusion.10
  18.1 8.4 fusion.118
  26.9 0.8 fusion.117
  28.6 1.9 select_add_fusion.10
  31.2 8.4 fusion.118
  41.7 1.9 select_add_fusion.10
  44.3 8.4 fusion.118
  53.3 49.2 %psum.70 = f32[15360]{0:T(1024)S(1)} all-reduce(f32[15360]{0:T(1024)S(1)} %reshape.226), channel_id=1, replica_groups=mesh['frame'=16,'dom'=8,'coef'=4] {'frame'}, use_global_device_ids=true, to_apply=%region_2.3 | all-reduce | flops 15360 | bytes 122880 | tf_op jit(solution)/shard_map/psum | solution.py:87
  102.5 35.2 %psum.71 = f32[15360]{0:T(1024)S(1)} all-reduce(f32[15360]{0:T(1024)S(1)} %psum.70), channel_id=1, replica_groups=mesh['frame'=16,'dom'=8,'coef'=4] {'dom'}, use_global_device_ids=true, to_apply=%region_3.4 | all-reduce | flops 15360 | bytes 122880 | tf_op jit(solution)/shard_map/psum | solution.py:87
  137.8 53.3 %while.54 = (s32[]{:T(128)}, f32[4096]{0:T(1024)S(1)}, s32[8,4096]{1,0:T(8,128)}, f32[8,4096]{1,0:T(8,128)}, f32[8,4096]{1,0:T(8,128)}, /*index=5*/s32[8,32]{1,0...) while((s32[]{:T(128)}, f32[4096]{0:T(1024)S(1)}, ...), condition=%wide.region_7.0_spmd, body=%wide.region_6.8_spmd.sunk | while | flops 30371208 | bytes 11859845 | solution.py:59
  139.6 4.2 select_add_fusion.8
  144.7 6.1 fusion.108
  151.2 0.8 fusion.106
  152.9 4.2 select_add_fusion.8
  158.1 6.1 fusion.108
  166.2 4.2 select_add_fusion.8
  171.4 6.1 fusion.108
  179.5 4.2 select_add_fusion.8
  184.7 6.1 fusion.108
  191.7 15.0 %all-reduce = (f32[4096]{0:T(1024)S(1)}, f32[]{:T(128)}) all-reduce(f32[4096]{0:T(1024)S(1)} %get-tuple-element.530, f32[]{:T(128)} %multiply_reduce_fusion.1), channel_id=1, replica_groups=mesh['frame'=16,'dom'=8,'coef'=4] {'coef'}, use_global_device_ids=true, to_apply=%region_8.10 | all-reduce | flops 4097 | bytes 32776 | tf_op jit(solution)/shard_map/psum | solution.py:100
  207.3 253.8 %psum.74 = f32[]{:T(128)} all-reduce(f32[]{:T(128)} %multiply_reduce_fusion.3), channel_id=1, replica_groups=mesh['frame'=16,'dom'=8,'coef'=4] {'frame','dom'}, use_global_device_ids=true, to_apply=%region_10.12 | all-reduce | flops 1 | bytes 8 | tf_op jit(solution)/shard_map/psum | solution.py:101
  462.5 49.7 %while.57 = (s32[]{:T(128)}, f32[96,160]{0,1:T(8,128)S(1)}, s32[8,32]{1,0:T(8,128)}, f32[4096]{0:T(1024)S(1)}, s32[8,4096]{1,0:T(8,128)}, /*index=5*/f32[8,4096]...) while((s32[]{:T(128)}, f32[96,160]{0,1:T(8,128)S(1)}, ...), condition=%wide.region_12.14_spmd.clone, body=%wide.region_11.13_spmd.clone.sunk | while | flops 42192900 | bytes 11854863 | solution.py:75
  464.2 1.9 select_add_fusion.11
  466.2 8.4 fusion.124
  476.7 1.9 select_add_fusion.11
  478.6 8.4 fusion.124
  489.1 1.9 select_add_fusion.11
  491.0 8.4 fusion.124
  501.5 1.9 select_add_fusion.11
  503.5 8.4 fusion.124
  512.4 39.3 %psum.75 = f32[15360]{0:T(1024)S(1)} all-reduce(f32[15360]{0:T(1024)S(1)} %reshape.228), channel_id=1, replica_groups=mesh['frame'=16,'dom'=8,'coef'=4] {'frame'}, use_global_device_ids=true, to_apply=%region_13.15 | all-reduce | flops 15360 | bytes 122880 | tf_op jit(solution)/shard_map/psum | solution.py:87
  551.8 34.9 %psum.76 = f32[15360]{0:T(1024)S(1)} all-reduce(f32[15360]{0:T(1024)S(1)} %psum.75), channel_id=1, replica_groups=mesh['frame'=16,'dom'=8,'coef'=4] {'dom'}, use_global_device_ids=true, to_apply=%region_14.16 | all-reduce | flops 15360 | bytes 122880 | tf_op jit(solution)/shard_map/psum | solution.py:87
  587.3 6.9 psum.77
  595.6 53.3 %while.55 = (s32[]{:T(128)}, f32[4096]{0:T(1024)S(1)}, s32[8,4096]{1,0:T(8,128)}, f32[8,4096]{1,0:T(8,128)}, f32[8,4096]{1,0:T(8,128)}, /*index=5*/s32[8,32]{1,0...) while((s32[]{:T(128)}, f32[4096]{0:T(1024)S(1)}, ...), condition=%wide.region_18.20_spmd, body=%wide.region_17.19_spmd.sunk | while | flops 30371208 | bytes 11859845 | solution.py:59
  597.4 4.2 select_add_fusion.9
  602.5 6.1 fusion.113
  610.7 4.2 select_add_fusion.9
  615.8 6.1 fusion.113
  624.0 4.2 select_add_fusion.9
  629.1 6.1 fusion.113
  637.3 4.2 select_add_fusion.9
  642.5 6.1 fusion.113
  648.9 12.1 %psum.78 = f32[4096]{0:T(1024)S(1)} all-reduce(f32[4096]{0:T(1024)S(1)} %get-tuple-element.532), channel_id=1, replica_groups=mesh['frame'=16,'dom'=8,'coef'=4] {'coef'}, use_global_device_ids=true, to_apply=%region_19.21 | all-reduce | flops 4096 | bytes 32768 | tf_op jit(solution)/shard_map/psum | solution.py:100
  661.6 255.7 %psum.79 = f32[]{:T(128)} all-reduce(f32[]{:T(128)} %multiply_reduce_fusion.2), channel_id=1, replica_groups=mesh['frame'=16,'dom'=8,'coef'=4] {'frame','dom'}, use_global_device_ids=true, to_apply=%region_21.23 | all-reduce | flops 1 | bytes 8 | tf_op jit(solution)/shard_map/psum | solution.py:101
  (283 shorter events, 44.0 us)
Async XLA Ops:
  4.3 9.1 copy-start
  17.4 9.1 copy-start
  30.5 9.1 copy-start
  43.6 9.1 copy-start
  137.8 324.6 %copy-start.4 = (f32[4096]{0:T(1024)S(1)}, f32[4096]{0:T(1024)}, u32[]{:S(2)}) copy-start(f32[4096]{0:T(1024)} %get-tuple-element.1094) | copy-start | bytes 49156
  137.9 6.0 copy-start.1
  151.2 6.0 copy-start.1
  164.5 6.0 copy-start.1
  177.8 6.0 copy-start.1
  466.1 8.4 copy-start.2
  478.6 8.4 copy-start.2
  491.0 8.4 copy-start.2
  503.4 8.4 copy-start.2
  595.6 6.0 copy-start.3
  608.9 6.0 copy-start.3
  622.3 6.0 copy-start.3
  635.6 6.0 copy-start.3
